TPU v7x, 32 devices: a whole 2x2x4 slice. The times are simulated.
32 devices in a mesh: req: 4 (over y, core), seq: 8 (over z, x).
Axes of the slice: x: 2, y: 2, z: 4, core: 2. Of those that a mesh axis runs over, the one named last changes fastest.
Arguments:
- embedded: bfloat16 [4, 48, 3584], P(None, 'req'), may hold values from -6 to 6
- cache_keys: bfloat16 [4, 4096, 2048], P('req', 'seq'), may hold values from -6 to 6
- cache_values: bfloat16 [4, 4096, 2048], P('req', 'seq'), may hold values from -6 to 6
- token_owner: int32 [4, 4096], P('req', 'seq'), may hold values from 0 to 11, as said below
- dealing: int32 [48], replicated, may hold values from 0 to 47, as said below
- lengths: int32 [48], replicated, may hold values from 1 to 2048, as said below
- project_weight: bfloat16 [3584, 8192], P(None, 'seq')
- output_weight: bfloat16 [4096, 3584], P('seq'), may hold values from -0.09375 to 0.09375
- gate_weight: bfloat16 [3584, 14336], P(None, ('req', 'seq')), may hold values from -0.09375 to 0.09375
- up_weight: bfloat16 [3584, 14336], P(None, ('req', 'seq')), may hold values from -0.09375 to 0.09375
- down_weight: bfloat16 [14336, 3584], P(('req', 'seq')), may hold values from -0.046875 to 0.046875
- gain_first: float32 [3584], replicated, may hold values from 0.1 to 1.9
- gain_second: float32 [3584], replicated, may hold values from 0.1 to 1.9
- gain_third: float32 [3584], replicated, may hold values from 0.1 to 1.9
- gain_fourth: float32 [3584], replicated, may hold values from 0.1 to 1.9
Outputs:
- results: bfloat16 [4, 48, 3584], P(None, 'req')
Inputs may be any that keep to these rules, and one draw needn't show every extreme that they name: A permutation of the requests; slot i of req group g serves request dealing[g * 12 + i]. The lengths of the 12 requests dealt to one group sum to 4096; in every group the longest is exactly 2048. `token_owner`: each slot owns a contiguous run of its group's pool, runs in slot order, as many tokens as its request's length.
All inputs are finite; a program needn't handle non-finite values.
Results may differ from a plain program's by a relative error of at most 0.012.
The roundings to bfloat16 on the way count: a program that leaves them out, or rounds other values in their place, can miss the bound.
Values may be sent and summed in bfloat16 or wider, within the bound.
A program may use at most 128 MiB of HBM per device.

v0:
```python
import math
import jax
import jax.numpy as jnp
from jax import lax
from jax.sharding import PartitionSpec as P

H = 16
KVH = 8
HD = 256
STEPS = 4
soft_cap = 50.0
epsilon = 1e-06


def rms_scale(values, gain):
    mean_square = jnp.mean(values * values, axis=-1, keepdims=True)
    return values * lax.rsqrt(mean_square + epsilon) * gain


def rotate(values, positions):
    half_width = values.shape[-1] // 2
    freq_index = jnp.arange(half_width, dtype=jnp.float32)
    inverse = jnp.exp(freq_index * (-2.0 * math.log(10000.0) / values.shape[-1]))
    angles = positions[:, None] * inverse[None, :]
    cosine = jnp.cos(angles)[:, None, :]
    sine = jnp.sin(angles)[:, None, :]
    first_half = values[..., :half_width]
    second_half = values[..., half_width:]
    return jnp.concatenate(
        [first_half * cosine - second_half * sine, second_half * cosine + first_half * sine],
        axis=-1,
    )


def capped_weight(scores):
    return jnp.exp(soft_cap * jnp.tanh(scores / soft_cap))


def rounded(values):
    return lax.optimization_barrier(values.astype(jnp.bfloat16)).astype(jnp.float32)


def body(
    embedded,
    cache_keys,
    cache_values,
    token_owner,
    dealing,
    lengths,
    project_weight,
    output_weight,
    gate_weight,
    up_weight,
    down_weight,
    gain_first,
    gain_second,
    gain_third,
    gain_fourth,
):
    row_count = embedded.shape[1]
    rows = STEPS * row_count
    width = embedded.shape[2]
    local_tokens = cache_keys.shape[1]
    value_width = cache_keys.shape[2]
    group_size = H // KVH
    attention_width = H * HD
    column_count = output_weight.shape[0]
    group_index = lax.axis_index("req")
    seq_index = lax.axis_index("seq")
    seq_size = lax.axis_size("seq")
    req_size = lax.axis_size("req")
    column_start = seq_index * column_count
    slot_requests = lax.dynamic_slice_in_dim(dealing, group_index * row_count, row_count)
    matches = slot_requests[:, None] == jnp.arange(dealing.shape[0], dtype=jnp.int32)[None, :]
    base_positions = jnp.sum(jnp.where(matches, lengths[None, :], 0), axis=1)
    positions = base_positions[None, :] + jnp.arange(STEPS, dtype=jnp.int32)[:, None]
    positions = positions.reshape(rows).astype(jnp.float32)
    key_pool = cache_keys[0].reshape(local_tokens, KVH, HD)
    value_pool = cache_values[0].reshape(local_tokens, KVH, HD)
    slots = jnp.tile(jnp.arange(row_count, dtype=jnp.int32), STEPS)
    moments = jnp.repeat(jnp.arange(STEPS, dtype=jnp.int32), row_count)
    owned_mask = token_owner[0][None, :] == slots[:, None]
    stream = embedded.reshape(rows, width).astype(jnp.float32)
    normed = rms_scale(stream, gain_first).astype(jnp.bfloat16)
    local_part = jnp.dot(normed, project_weight, preferred_element_type=jnp.float32).astype(
        jnp.bfloat16
    )
    projected = lax.all_gather(local_part, "seq", axis=1, tiled=True)
    query_rows = projected[:, :attention_width].astype(jnp.float32).reshape(rows, H, HD)
    queries = (rotate(query_rows, positions) * HD ** (-0.5)).astype(jnp.bfloat16)
    key_rows = (
        projected[:, attention_width : attention_width + value_width]
        .astype(jnp.float32)
        .reshape(rows, KVH, HD)
    )
    fresh_keys = rotate(key_rows, positions).astype(jnp.bfloat16)
    fresh_values = projected[:, attention_width + value_width :].reshape(rows, KVH, HD)
    grouped = queries.reshape(rows, KVH, group_size, HD)
    all_keys = jnp.concatenate([key_pool, fresh_keys], axis=0)
    all_values = jnp.concatenate([value_pool, fresh_values], axis=0)
    fresh_mask = (
        (slots[None, :] == slots[:, None])
        & (moments[None, :] <= moments[:, None])
        & (seq_index == 0)
    )
    mask = jnp.concatenate([owned_mask, fresh_mask], axis=1)
    scores = jnp.einsum("igqd,tgd->igqt", grouped, all_keys, preferred_element_type=jnp.float32)
    weights = jnp.where(mask[:, None, None, :], capped_weight(scores), 0.0)
    totals = lax.psum(jnp.sum(weights, axis=-1), "seq").reshape(rows, H)
    outputs = jnp.einsum(
        "igqt,tgd->igqd",
        weights.astype(jnp.bfloat16),
        all_values,
        preferred_element_type=jnp.float32,
    ).reshape(rows, attention_width)
    outputs = lax.psum_scatter(outputs, "seq", scatter_dimension=1, tiled=True)
    spread = jnp.repeat(totals, HD, axis=1)
    spread = lax.dynamic_slice_in_dim(spread, column_start, column_count, 1)
    attended = (outputs / spread).astype(jnp.bfloat16)
    partial = jnp.dot(attended, output_weight, preferred_element_type=jnp.float32)
    mixed = lax.psum(partial, "seq")
    middle = stream + rms_scale(mixed, gain_second)
    feed_input = rms_scale(middle, gain_third).astype(jnp.bfloat16)
    block_rows = lax.all_gather(feed_input, "req", axis=0, tiled=True)
    gate_part = jnp.dot(block_rows, gate_weight, preferred_element_type=jnp.float32)
    up_part = jnp.dot(block_rows, up_weight, preferred_element_type=jnp.float32)
    hidden = (jax.nn.gelu(gate_part, approximate=True) * up_part).astype(jnp.bfloat16)
    summed = jnp.dot(hidden, down_weight, preferred_element_type=jnp.float32)
    summed = lax.psum_scatter(summed, "req", scatter_dimension=0, tiled=True)
    summed = lax.psum(summed, "seq")
    results = (middle + rms_scale(summed, gain_fourth)).astype(jnp.bfloat16)
    return results.reshape(STEPS, row_count, width)


def solution(mesh):
    return jax.shard_map(
        body,
        mesh=mesh,
        in_specs=(
            P(None, "req", None),
            P("req", "seq", None),
            P("req", "seq", None),
            P("req", "seq"),
            P(),
            P(),
            P(None, "seq"),
            P("seq", None),
            P(None, ("req", "seq")),
            P(None, ("req", "seq")),
            P(("req", "seq"), None),
            P(),
            P(),
            P(),
            P(),
        ),
        out_specs=P(None, "req", None),
        check_vma=False,
    )
```

profile of v0, /device:TPU:0, one launch (start us, length us, event | category | flops | bytes accessed | tf_op | source)
XLA Modules:
  0.0 383.3 jit_solution(17114336762805842567)
XLA Ops:
  6.6 2.1 copy.64
  9.9 2.1 reshape.160
  12.2 4.8 %convolution_convert_fusion = bf16[48,1024]{1,0:T(8,128)(2,1)S(1)} fusion(bf16[3584,1024]{1,0:T(8,128)(2,1)} %param.21, f32[48,3584]{1,0:T(8,128)} %reshape.160, f32[3584]{0:T(1024)S(1)} %copy-done.4, f32[48]{0:T(128)S(1)} %rsqrt.36), kind=kOutput, calls=%fused_computation.14 | convolution fusion | flops 352886784 | bytes 8140992 | tf_op jit(solution)/shard_map/dot_general | solution.py:85
  17.0 33.8 %all_gather.6 = bf16[48,8192]{1,0:T(8,128)(2,1)S(1)} all-gather(bf16[48,1024]{1,0:T(8,128)(2,1)S(1)} %convolution_convert_fusion), channel_id=1, replica_groups=mesh['req'=4,'seq'=8] {'seq'}, dimensions={1}, use_global_device_ids=true | all-gather | bytes 884736 | tf_op jit(solution)/shard_map/all_gather | solution.py:88
  58.6 3.9 %copy.69 = bf16[1,512,2048]{1,2,0:T(8,128)(2,1)} copy(bf16[1,512,2048]{2,1,0:T(8,128)(2,1)} %param.16) | data formatting | bytes 4194304 | tf_op args[1]
  62.6 3.9 %copy.72 = bf16[512,8,256]{2,0,1:T(8,128)(2,1)} copy(bf16[512,8,256]{0,2,1:T(8,128)(2,1)} %bitcast.44) | data formatting | bytes 4194304 | tf_op jit(solution)/shard_map/reshape;squeeze | solution.py:78
  66.5 1.6 copy.92
  68.1 3.9 %copy.65 = bf16[1,512,2048]{1,2,0:T(8,128)(2,1)} copy(bf16[1,512,2048]{2,1,0:T(8,128)(2,1)} %param.17) | data formatting | bytes 4194304 | tf_op args[2]
  72.0 3.9 %copy.67 = bf16[512,8,256]{2,0,1:T(8,128)(2,1)} copy(bf16[512,8,256]{0,2,1:T(8,128)(2,1)} %bitcast.45) | data formatting | bytes 4194304 | tf_op jit(solution)/shard_map/reshape;squeeze | solution.py:79
  77.0 2.9 fusion.40
  80.5 1.5 copy.75
  82.1 2.6 reshape.156
  84.8 21.7 %psum.21 = f32[48,16]{0,1:T(8,128)S(1)} all-reduce(f32[48,16]{0,1:T(8,128)S(1)} %bitcast.56), channel_id=1, replica_groups=mesh['req'=4,'seq'=8] {'seq'}, use_global_device_ids=true, to_apply=%region_4.5 | all-reduce | flops 768 | bytes 6144 | tf_op jit(solution)/shard_map/psum | solution.py:109
  108.1 40.9 %reduce-scatter.3.cloned.1.call-done = f32[48,512]{1,0:T(8,128)} async-done(((f32[48,4096]{1,0:T(8,128)}), f32[48,512]{1,0:T(8,128)}) %reduce-scatter.3.cloned.1.call-update) | async-done | bytes 98320 | tf_op jit(solution)/shard_map/reduce_scatter | solution.py:116
  149.0 3.8 fusion.29
  152.8 72.8 %all-reduce.3.cloned.1.call-done = f32[48,3584]{1,0:T(8,128)} async-done(((f32[48,3584]{1,0:T(8,128)}), f32[48,3584]{1,0:T(8,128)}) %all-reduce.3.cloned.1.call-update) | async-done | bytes 688144 | tf_op jit(solution)/shard_map/psum | solution.py:121
  226.9 1.6 multiply_reduce_fusion.1
  230.3 17.7 %all-gather.2.cloned.1.call-done = bf16[192,3584]{1,0:T(8,128)(2,1)} async-done(((bf16[48,3584]{1,0:T(8,128)(2,1)}), bf16[192,3584]{1,0:T(8,128)(2,1)}) %all-gather.2.cloned.1.call-update) | async-done | bytes 1376272 | tf_op jit(solution)/shard_map/all_gather | solution.py:124
  247.9 4.1 %fusion.41 = f32[192,448]{1,0:T(8,128)} fusion(bf16[192,3584]{1,0:T(8,128)(2,1)} %all-gather.2.cloned.1.call-done, bf16[3584,448]{0,1:T(8,128)(2,1)} %param.23), kind=kOutput, calls=%fused_computation.75 | convolution fusion | flops 616562688 | bytes 4931584 | tf_op jit(solution)/shard_map/dot_general | solution.py:125
  252.1 6.0 %fusion.10 = f32[192,3584]{1,0:T(8,128)} fusion(bf16[448,3584]{1,0:T(8,128)(2,1)S(1)} %copy-done, bf16[192,3584]{1,0:T(8,128)(2,1)} %all-gather.2.cloned.1.call-done, bf16[3584,448]{0,1:T(8,128)(2,1)} %param.24, f32[192,448]{1,0:T(8,128)} %fusion.41), kind=kOutput, calls=%fused_computation.15 | convolution fusion | flops 1233985536 | bytes 10895360 | tf_op jit(solution)/shard_map/dot_general | solution.py:128
  258.2 35.6 %reduce-scatter.5.cloned.1.call-done = f32[48,3584]{1,0:T(8,128)} async-done(((f32[192,3584]{1,0:T(8,128)}), f32[48,3584]{1,0:T(8,128)}) %reduce-scatter.5.cloned.1.call-update) | async-done | bytes 688144 | tf_op jit(solution)/shard_map/reduce_scatter | solution.py:129
  293.8 77.4 %all-reduce.5.cloned.1.call-done = f32[48,3584]{1,0:T(8,128)} async-done(((f32[48,3584]{1,0:T(8,128)}), f32[48,3584]{1,0:T(8,128)}) %all-reduce.5.cloned.1.call-update) | async-done | bytes 688144 | tf_op jit(solution)/shard_map/psum | solution.py:130
  372.4 1.5 add_convert_fusion
  374.7 2.0 copy.77
  (68 shorter events, 17.7 us)
Async XLA Ops:
  6.5 245.5 %copy-start = (bf16[448,3584]{1,0:T(8,128)(2,1)S(1)}, bf16[448,3584]{1,0:T(8,128)(2,1)}, u32[]{:S(2)}) copy-start(bf16[448,3584]{1,0:T(8,128)(2,1)} %param.25) | copy-start | bytes 9633796
  6.5 5.7 %copy-start.4 = (f32[3584]{0:T(1024)S(1)}, f32[3584]{0:T(1024)}, u32[]{:S(2)}) copy-start(f32[3584]{0:T(1024)} %param.26) | copy-start | bytes 43012
  6.5 142.4 %reduce-scatter.3.cloned.1.call-start = ((), (), s32[]{:S(2)}) async-start(), calls=%async_computation.2 | async-start | bytes 884736 | tf_op jit(solution)/shard_map/reduce_scatter | solution.py:116
  17.0 35.6 %copy-start.8 = (s32[48]{0:T(128)S(1)}, s32[48]{0:T(128)}, u32[]{:S(2)}) copy-start(s32[48]{0:T(128)} %param.19) | copy-start | bytes 580
  17.0 35.7 %copy-start.9 = (s32[48]{0:T(128)S(1)}, s32[48]{0:T(128)}, u32[]{:S(2)}) copy-start(s32[48]{0:T(128)} %param.20) | copy-start | bytes 580
  54.9 3.6 copy-start.7
  77.0 2.9 copy-start.2
  77.0 2.9 copy-start.3
  84.7 140.9 %all-reduce.3.cloned.1.call-start = ((), (), s32[]{:S(2)}) async-start(), calls=%async_computation.3 | async-start | bytes 1376256 | tf_op jit(solution)/shard_map/psum | solution.py:121
  149.0 77.9 %copy-start.6 = (f32[3584]{0:T(1024)S(1)}, f32[3584]{0:T(1024)}, u32[]{:S(2)}) copy-start(f32[3584]{0:T(1024)} %param.27) | copy-start | bytes 43012
  152.7 76.6 %copy-start.5 = (f32[3584]{0:T(1024)S(1)}, f32[3584]{0:T(1024)}, u32[]{:S(2)}) copy-start(f32[3584]{0:T(1024)} %param.28) | copy-start | bytes 43012
  152.7 95.2 %all-gather.2.cloned.1.call-start = ((), (), s32[]{:S(2)}) async-start(), calls=%async_computation.4 | async-start | bytes 1720320 | tf_op jit(solution)/shard_map/all_gather | solution.py:124
  228.4 0.9 copy-start.1
  230.2 63.5 %reduce-scatter.5.cloned.1.call-start = ((), (), s32[]{:S(2)}) async-start(), calls=%async_computation.5 | async-start | bytes 3440640 | tf_op jit(solution)/shard_map/reduce_scatter | solution.py:129
  258.1 113.0 %all-reduce.5.cloned.1.call-start = ((), (), s32[]{:S(2)}) async-start(), calls=%async_computation.6 | async-start | bytes 1376256 | tf_op jit(solution)/shard_map/psum | solution.py:130
Sparse Core Ops, SparseCore 0:
  84.8 64.0 reduce-scatter.2
  152.9 72.6 all-reduce.2
  230.3 17.5 all-gather.1
  258.2 35.4 reduce-scatter.4
  297.4 73.6 all-reduce.4
where the time goes:
time: 384 us; the launch traced here: 383 us
  waiting for transfers between devices  244 us (64%)
  blocking collectives  55.5 us (14%)
  local copies, waits for them, and re-layouts  36.6 us (10%)
  matrix products  22.2 us (6%)
  between operations  13.3 us (3%)
  other arithmetic  11.1 us (3%)
    psum x1, waiting for transfers between devices, body(): summed = lax.psum(summed, 'seq')  77.4 us
    psum x1, waiting for transfers between devices, body(): mixed = lax.psum(partial, 'seq')  72.8 us
    reduce_scatter x1, waiting for transfers between devices, body(): outputs = lax.psum_scatter(outputs, 'seq', scatter_dimension=1, tiled=True)  40.9 us
    reduce_scatter x1, waiting for transfers between devices, body(): summed = lax.psum_scatter(summed, 'req', scatter_dimension=0, tiled=True)  35.6 us
    all_gather x1, blocking collectives, body(): projected = lax.all_gather(local_part, 'seq', axis=1, tiled=True)  33.8 us
    psum x1, blocking collectives, body(): totals = lax.psum(jnp.sum(weights, axis=-1), 'seq').reshape(rows, H)  21.7 us
    all_gather x1, waiting for transfers between devices, body(): block_rows = lax.all_gather(feed_input, 'req', axis=0, tiled=True)  17.7 us
    unnamed x26, local copies, waits for them, and re-layouts  12.7 us
  transfers between devices with their start and end apart: 5, of which 5 were waited for; matrix products, arithmetic and copies ran while one was open for 0% of the time, Pallas kernels for 0%

commit v1 on v0

--- a/solution.py
+++ b/solution.py
@@ -85,7 +85,15 @@
     local_part = jnp.dot(normed, project_weight, preferred_element_type=jnp.float32).astype(
         jnp.bfloat16
     )
-    projected = lax.all_gather(local_part, "seq", axis=1, tiled=True)
+    ways, here = (lax.axis_size("seq"), lax.axis_index("seq"))
+    grown, reach = (local_part, 1)
+    while reach < ways:
+        theirs = lax.ppermute(grown, "seq", [(d, d ^ reach) for d in range(ways)])
+        mine_first = jnp.concatenate([grown, theirs], axis=1)
+        theirs_first = jnp.concatenate([theirs, grown], axis=1)
+        grown = jnp.where(here & reach == 0, mine_first, theirs_first)
+        reach = 2 * reach
+    projected = grown
     query_rows = projected[:, :attention_width].astype(jnp.float32).reshape(rows, H, HD)
     queries = (rotate(query_rows, positions) * HD ** (-0.5)).astype(jnp.bfloat16)
     key_rows = (

time: 384 us -> 358 us (0.932)
  blocking collectives: 55.5 us -> 21 us
  starting transfers between devices: 0.17 us -> 7.65 us
  waiting for transfers between devices: 244 us -> 251 us
  local copies, waits for them, and re-layouts: 36.6 us -> 32.3 us
    all_gather x1 -> x0, blocking collectives: 33.8 us -> none  [body(): projected = lax.all_gather(local_part, 'seq', axis=1, tiled=True)]
    ppermute x0 -> x3, starting transfers between devices: none -> 7.48 us  [body(): theirs = lax.ppermute(grown, 'seq', [(d, d ^ reach) for d in range(ways)])]
    ppermute x0 -> x3, waiting for transfers between devices: none -> 6.9 us  [body(): theirs = lax.ppermute(grown, 'seq', [(d, d ^ reach) for d in range(ways)])]
  transfers between devices with their start and end apart: 5 -> 8, of which waited for: 5 -> 8; matrix products, arithmetic and copies ran while one was open for 0% -> 5% of each run, Pallas kernels for 0% -> 0%
where the time goes in v1:
time: 358 us; the launch traced here: 357 us
  waiting for transfers between devices  251 us (70%)
  local copies, waits for them, and re-layouts  32.3 us (9%)
  blocking collectives  21 us (6%)
  matrix products  20.3 us (6%)
  between operations  13.4 us (4%)
  other arithmetic  11 us (3%)
  starting transfers between devices  7.65 us (2%)
    psum x1, waiting for transfers between devices, body(): summed = lax.psum(summed, 'seq')  77.4 us
    psum x1, waiting for transfers between devices, body(): mixed = lax.psum(partial, 'seq')  72.8 us
    reduce_scatter x1, waiting for transfers between devices, body(): outputs = lax.psum_scatter(outputs, 'seq', scatter_dimension=1, tiled=True)  40.8 us
    reduce_scatter x1, waiting for transfers between devices, body(): summed = lax.psum_scatter(summed, 'req', scatter_dimension=0, tiled=True)  35.6 us
    psum x1, blocking collectives, body(): totals = lax.psum(jnp.sum(weights, axis=-1), 'seq').reshape(rows, H)  21 us
    all_gather x1, waiting for transfers between devices, body(): block_rows = lax.all_gather(feed_input, 'req', axis=0, tiled=True)  17.7 us
    unnamed x26, local copies, waits for them, and re-layouts  12.2 us
    ppermute x3, starting transfers between devices, body(): theirs = lax.ppermute(grown, 'seq', [(d, d ^ reach) for d in range(ways)])  7.48 us
  transfers between devices with their start and end apart: 8, of which 8 were waited for; matrix products, arithmetic and copies ran while one was open for 5% of the time, Pallas kernels for 0%

profile of v1, /device:TPU:0, one launch (start us, length us, event | category | flops | bytes accessed | tf_op | source)
XLA Modules:
  0.0 356.8 jit_solution(6538524719189028177)
XLA Ops:
  6.5 2.1 copy.64
  9.9 2.1 reshape.160
  12.2 4.8 %convolution_convert_fusion = bf16[48,1024]{1,0:T(8,128)(2,1)S(1)} fusion(bf16[3584,1024]{1,0:T(8,128)(2,1)} %param.21, f32[48,3584]{1,0:T(8,128)} %reshape.160, f32[3584]{0:T(1024)S(1)} %copy-done.4, f32[48]{0:T(128)S(1)} %rsqrt.36), kind=kOutput, calls=%fused_computation.14 | convolution fusion | flops 352886784 | bytes 8140992 | tf_op jit(solution)/shard_map/dot_general | solution.py:85
  17.0 3.0 collective-permute-start
  20.8 2.1 collective-permute-done
  22.9 2.0 collective-permute-start.1
  24.9 4.2 %collective-permute-done.1 = bf16[48,2048]{1,0:T(8,128)(2,1)S(1)} collective-permute-done((bf16[48,2048]{1,0:T(8,128)(2,1)S(1)}, bf16[48,2048]{1,0:T(8,128)(2,1)S(1)}, u32[]{:S(2)}, u32[]{:S(2)}) %collective-permute-start.1) | collective-permute-done | bytes 196640 | tf_op jit(solution)/shard_map/ppermute | solution.py:91
  29.9 2.5 collective-permute-start.2
  32.4 3.9 %copy.69 = bf16[1,512,2048]{1,2,0:T(8,128)(2,1)} copy(bf16[1,512,2048]{2,1,0:T(8,128)(2,1)} %param.16) | data formatting | bytes 4194304 | tf_op args[1]
  36.3 3.9 %copy.72 = bf16[512,8,256]{2,0,1:T(8,128)(2,1)} copy(bf16[512,8,256]{0,2,1:T(8,128)(2,1)} %bitcast.44) | data formatting | bytes 4194304 | tf_op jit(solution)/shard_map/reshape;squeeze | solution.py:78
  40.2 3.9 %copy.65 = bf16[1,512,2048]{1,2,0:T(8,128)(2,1)} copy(bf16[1,512,2048]{2,1,0:T(8,128)(2,1)} %param.17) | data formatting | bytes 4194304 | tf_op args[2]
  44.2 3.9 %copy.67 = bf16[512,8,256]{2,0,1:T(8,128)(2,1)} copy(bf16[512,8,256]{0,2,1:T(8,128)(2,1)} %bitcast.45) | data formatting | bytes 4194304 | tf_op jit(solution)/shard_map/reshape;squeeze | solution.py:79
  48.9 1.6 maximum_select_fusion
  56.3 2.7 reshape.156
  59.1 21.0 %psum.21 = f32[48,16]{0,1:T(8,128)S(1)} all-reduce(f32[48,16]{0,1:T(8,128)S(1)} %bitcast.56), channel_id=1, replica_groups=mesh['req'=4,'seq'=8] {'seq'}, use_global_device_ids=true, to_apply=%region_4.5 | all-reduce | flops 768 | bytes 6144 | tf_op jit(solution)/shard_map/psum | solution.py:117
  81.7 40.8 %reduce-scatter.3.cloned.1.call-done = f32[48,512]{1,0:T(8,128)} async-done(((f32[48,4096]{1,0:T(8,128)}), f32[48,512]{1,0:T(8,128)}) %reduce-scatter.3.cloned.1.call-update) | async-done | bytes 98320 | tf_op jit(solution)/shard_map/reduce_scatter | solution.py:124
  122.5 3.8 %fusion.29 = f32[48,3584]{1,0:T(8,128)} fusion(bf16[512,3584]{1,0:T(8,128)(2,1)} %param.22, f32[48,512]{1,0:T(8,128)} %reduce-scatter.3.cloned.1.call-done, f32[48,4096]{1,0:T(8,128)} %bitcast.51, s32[]{:T(128)S(6)} %select_n.47), kind=kOutput, calls=%fused_computation.54 | convolution fusion | flops 176209920 | bytes 4554756 | tf_op jit(solution)/shard_map/dot_general | solution.py:128
  126.3 72.8 %all-reduce.3.cloned.1.call-done = f32[48,3584]{1,0:T(8,128)} async-done(((f32[48,3584]{1,0:T(8,128)}), f32[48,3584]{1,0:T(8,128)}) %all-reduce.3.cloned.1.call-update) | async-done | bytes 688144 | tf_op jit(solution)/shard_map/psum | solution.py:129
  203.8 17.7 %all-gather.2.cloned.1.call-done = bf16[192,3584]{1,0:T(8,128)(2,1)} async-done(((bf16[48,3584]{1,0:T(8,128)(2,1)}), bf16[192,3584]{1,0:T(8,128)(2,1)}) %all-gather.2.cloned.1.call-update) | async-done | bytes 1376272 | tf_op jit(solution)/shard_map/all_gather | solution.py:132
  221.5 4.2 %fusion.41 = f32[192,448]{1,0:T(8,128)} fusion(bf16[192,3584]{1,0:T(8,128)(2,1)} %all-gather.2.cloned.1.call-done, bf16[3584,448]{0,1:T(8,128)(2,1)} %param.23), kind=kOutput, calls=%fused_computation.78 | convolution fusion | flops 616562688 | bytes 4931584 | tf_op jit(solution)/shard_map/dot_general | solution.py:133
  225.6 6.0 %fusion.10 = f32[192,3584]{1,0:T(8,128)} fusion(bf16[448,3584]{1,0:T(8,128)(2,1)S(1)} %copy-done, bf16[192,3584]{1,0:T(8,128)(2,1)} %all-gather.2.cloned.1.call-done, bf16[3584,448]{0,1:T(8,128)(2,1)} %param.24, f32[192,448]{1,0:T(8,128)} %fusion.41), kind=kOutput, calls=%fused_computation.15 | convolution fusion | flops 1233985536 | bytes 10895360 | tf_op jit(solution)/shard_map/dot_general | solution.py:136
  231.7 35.6 %reduce-scatter.5.cloned.1.call-done = f32[48,3584]{1,0:T(8,128)} async-done(((f32[192,3584]{1,0:T(8,128)}), f32[48,3584]{1,0:T(8,128)}) %reduce-scatter.5.cloned.1.call-update) | async-done | bytes 688144 | tf_op jit(solution)/shard_map/reduce_scatter | solution.py:137
  267.3 77.4 %all-reduce.5.cloned.1.call-done = f32[48,3584]{1,0:T(8,128)} async-done(((f32[48,3584]{1,0:T(8,128)}), f32[48,3584]{1,0:T(8,128)}) %all-reduce.5.cloned.1.call-update) | async-done | bytes 688144 | tf_op jit(solution)/shard_map/psum | solution.py:138
  348.3 2.0 copy.77
  (76 shorter events, 19.6 us)
Async XLA Ops:
  6.5 219.1 %copy-start = (bf16[448,3584]{1,0:T(8,128)(2,1)S(1)}, bf16[448,3584]{1,0:T(8,128)(2,1)}, u32[]{:S(2)}) copy-start(bf16[448,3584]{1,0:T(8,128)(2,1)} %param.25) | copy-start | bytes 9633796
  6.5 5.7 %copy-start.4 = (f32[3584]{0:T(1024)S(1)}, f32[3584]{0:T(1024)}, u32[]{:S(2)}) copy-start(f32[3584]{0:T(1024)} %param.26) | copy-start | bytes 43012
  6.5 115.9 %reduce-scatter.3.cloned.1.call-start = ((), (), s32[]{:S(2)}) async-start(), calls=%async_computation.2 | async-start | bytes 884736 | tf_op jit(solution)/shard_map/reduce_scatter | solution.py:124
  12.2 8.0 %copy-start.8 = (s32[48]{0:T(128)S(1)}, s32[48]{0:T(128)}, u32[]{:S(2)}) copy-start(s32[48]{0:T(128)} %param.19) | copy-start | bytes 580
  12.2 8.1 %copy-start.7 = (s32[1,512]{1,0:T(1,128)S(1)}, s32[1,512]{1,0:T(1,128)}, u32[]{:S(2)}) copy-start(s32[1,512]{1,0:T(1,128)} %param.18) | copy-start | bytes 6148
  12.2 8.2 %copy-start.9 = (s32[48]{0:T(128)S(1)}, s32[48]{0:T(128)}, u32[]{:S(2)}) copy-start(s32[48]{0:T(128)} %param.20) | copy-start | bytes 580
  17.0 5.8 %collective-permute-start = (bf16[48,1024]{1,0:T(8,128)(2,1)S(1)}, bf16[48,1024]{1,0:T(8,128)(2,1)S(1)}, u32[]{:S(2)}, u32[]{:S(2)}) collective-permute-start(bf16[48,1024]{1,0:T(8,128)(2,1)S(1)} %convolution_convert_fusion), channel_id=1, source_target_pairs={{0,1},{1,0},{2,3},{3,2},{4,5},{5,4},{6,7},{7,6},{8,9},{9,8},{10,11... | collective-permute-start | bytes 294920 | tf_op jit(solution)/shard_map/ppermute | solution.py:91
  22.9 6.2 %collective-permute-start.1 = (bf16[48,2048]{1,0:T(8,128)(2,1)S(1)}, bf16[48,2048]{1,0:T(8,128)(2,1)S(1)}, u32[]{:S(2)}, u32[]{:S(2)}) collective-permute-start(bf16[48,2048]{1,0:T(8,128)(2,1)S(1)} %maximum_select_fusion.2), channel_id=1, source_target_pairs={{0,2},{1,3},{2,0},{3,1},{4,6},{5,7},{6,4},{7,5},{8,10},{9,11},{10,... | collective-permute-start | bytes 589832 | tf_op jit(solution)/shard_map/ppermute | solution.py:91
  29.9 19.0 %collective-permute-start.2 = (bf16[48,4096]{1,0:T(8,128)(2,1)}, bf16[48,4096]{1,0:T(8,128)(2,1)}, u32[]{:S(2)}, u32[]{:S(2)}) collective-permute-start(bf16[48,4096]{1,0:T(8,128)(2,1)} %maximum_select_fusion.1), channel_id=1, source_target_pairs={{0,4},{1,5},{2,6},{3,7},{4,0},{5,1},{6,2},{7,3},{8,12},{9,13},{10,... | collective-permute-start | bytes 1179656 | tf_op jit(solution)/shard_map/ppermute | solution.py:91
  51.1 1.6 copy-start.3
  52.7 1.6 copy-start.2
  59.0 140.1 %all-reduce.3.cloned.1.call-start = ((), (), s32[]{:S(2)}) async-start(), calls=%async_computation.3 | async-start | bytes 1376256 | tf_op jit(solution)/shard_map/psum | solution.py:129
  122.5 77.9 %copy-start.6 = (f32[3584]{0:T(1024)S(1)}, f32[3584]{0:T(1024)}, u32[]{:S(2)}) copy-start(f32[3584]{0:T(1024)} %param.27) | copy-start | bytes 43012
  126.2 76.6 %copy-start.5 = (f32[3584]{0:T(1024)S(1)}, f32[3584]{0:T(1024)}, u32[]{:S(2)}) copy-start(f32[3584]{0:T(1024)} %param.28) | copy-start | bytes 43012
  126.3 95.2 %all-gather.2.cloned.1.call-start = ((), (), s32[]{:S(2)}) async-start(), calls=%async_computation.4 | async-start | bytes 1720320 | tf_op jit(solution)/shard_map/all_gather | solution.py:132
  202.0 0.9 copy-start.1
  203.8 63.5 %reduce-scatter.5.cloned.1.call-start = ((), (), s32[]{:S(2)}) async-start(), calls=%async_computation.5 | async-start | bytes 3440640 | tf_op jit(solution)/shard_map/reduce_scatter | solution.py:137
  231.7 113.0 %all-reduce.5.cloned.1.call-start = ((), (), s32[]{:S(2)}) async-start(), calls=%async_computation.6 | async-start | bytes 1376256 | tf_op jit(solution)/shard_map/psum | solution.py:138
Sparse Core Ops, SparseCore 0:
  59.1 63.2 reduce-scatter.2
  126.4 72.7 all-reduce.2
  203.9 17.5 all-gather.1
  231.8 35.4 reduce-scatter.4
  270.9 73.6 all-reduce.4
